TPU v7x, 32 devices: a whole 2x2x4 slice. The times are simulated.
32 devices in a mesh: grp: 2 (over x), tm: 8 (over z, y), head: 2 (over core).
Axes of the slice: x: 2, y: 2, z: 4, core: 2. Of those that a mesh axis runs over, the one named last changes fastest.
Arguments:
- queries: bfloat16 [2048, 6144], P(('grp', 'tm'), 'head'), parts along dimension 0, may hold values from -130 to 130
- keys: bfloat16 [2048, 1024], P(('grp', 'tm'), 'head'), parts along dimension 0, may hold values from -7 to 7
- values: bfloat16 [2048, 1024], P(('grp', 'tm'), 'head'), parts along dimension 0, may hold values from -6 to 6
- span_mask: int32 [8, 4], P('grp'), parts along dimension 0, may hold values from 0 to 1, as said below
- section: int32 [8], P('grp'), parts along dimension 0, may hold values from 0 to 3
- section_gate: float32 [4, 6144], P(None, 'head'), may hold values from 0.1 to 1.9
Outputs:
- mixed: bfloat16 [2048, 6144], P(('grp', 'tm'), 'head'), parts along dimension 0
- log_total: float32 [48, 2048], P('head', ('grp', 'tm')), parts along dimension 1
There are 2 independent parts, one for each index of `grp`. A program takes and returns all parts, laid end to end along the dimension named above; an argument that names none is the same for every part. Nothing has to cross between parts.
Inputs may be any that keep to these rules, and one draw needn't show every extreme that they name: `span_mask`: the first column and the diagonal are 1 and everything above the diagonal is 0.
All inputs are finite; a program needn't handle non-finite values.
Results may differ from a plain program's by a relative error of at most 0.006.
Values may be sent and summed in bfloat16 or wider, within the bound.
A program may use at most 64 MiB of HBM per device.

v0:
```python
import math

import jax
import jax.numpy as jnp
from jax import lax
from jax.sharding import PartitionSpec as P

HEAD_SIZE = 128
CH = 256


neg_fill = -1e30


def from_behind(value, axis, steps):
    count = lax.axis_size(axis)
    pairs = [(source, (source + steps) % count) for source in range(count)]
    return lax.ppermute(value, axis, pairs)


def attend_block(carry, grouped, key_block, value_block, allowed, scale):
    run_max, run_total, accum = carry
    kv_heads = run_max.shape[0]
    key_rows = key_block.shape[0]
    keys_three = key_block.reshape(key_rows, kv_heads, HEAD_SIZE)
    values_three = value_block.reshape(key_rows, kv_heads, HEAD_SIZE)
    score = (
        jnp.einsum("qkgd,nkd->kgqn", grouped, keys_three, preferred_element_type=jnp.float32)
        * scale
    )
    score = jnp.where(allowed[None, None], score, neg_fill)
    new_max = jnp.maximum(run_max, jnp.max(score, axis=-1))
    weight = jnp.where(allowed[None, None], jnp.exp(score - new_max[..., None]), 0.0)
    factor = jnp.exp(run_max - new_max)
    new_total = run_total * factor + jnp.sum(weight, axis=-1)
    new_accum = accum * factor[..., None] + jnp.einsum(
        "kgqn,nkd->kgqd",
        weight.astype(jnp.bfloat16),
        values_three,
        preferred_element_type=jnp.float32,
    )
    return (new_max, new_total, new_accum)


def visit_block(carry, grouped, key_block, value_block, allowed, scale):
    return attend_block(carry, grouped, key_block, value_block, allowed, scale)


def on_device(queries, keys, values, span_mask, section, section_gate):
    tok_rows = queries.shape[0]
    kv_local = keys.shape[1] // HEAD_SIZE
    q_local = queries.shape[1] // HEAD_SIZE
    query_group = q_local // kv_local
    scale = 1.0 / math.sqrt(HEAD_SIZE)
    count = lax.axis_size("tm")
    here = lax.axis_index("tm")
    row_ids = jnp.arange(tok_rows, dtype=jnp.int32)
    global_rows = here * tok_rows + row_ids
    query_spans = global_rows // CH
    row_mask = jnp.take(span_mask, query_spans, axis=0)
    grouped = queries.reshape(tok_rows, kv_local, query_group, HEAD_SIZE)
    carry = (
        jnp.full((kv_local, query_group, tok_rows), neg_fill, jnp.float32),
        jnp.zeros((kv_local, query_group, tok_rows), jnp.float32),
        jnp.zeros((kv_local, query_group, tok_rows, HEAD_SIZE), jnp.float32),
    )
    local_spans = (here * tok_rows + row_ids) // CH
    carry = visit_block(
        carry, grouped, keys, values, jnp.take(row_mask, local_spans, axis=1) > 0, scale
    )

    def hop(step, state):
        stacked, inner = state
        stacked = from_behind(stacked, "tm", 1)
        source = (here - step) % count
        key_spans = (source * tok_rows + row_ids) // CH
        inner = visit_block(
            inner, grouped, stacked[0], stacked[1], jnp.take(row_mask, key_spans, axis=1) > 0, scale
        )
        return (stacked, inner)

    stacked, carry = lax.fori_loop(1, count, hop, (jnp.stack([keys, values]), carry))
    run_max, run_total, accum = carry
    attended = jnp.transpose(accum / run_total[..., None], (2, 0, 1, 3)).reshape(
        tok_rows, q_local * HEAD_SIZE
    )
    log_total = (run_max + jnp.log(run_total)).reshape(q_local, tok_rows)
    gate_rows = jnp.take(section_gate, jnp.take(section, query_spans), axis=0)
    mixed = (gate_rows * attended).astype(jnp.bfloat16)
    return (mixed, log_total)


def solution(mesh):
    placed = (
        P(("grp", "tm"), "head"),
        P(("grp", "tm"), "head"),
        P(("grp", "tm"), "head"),
        P("grp", None),
        P("grp"),
        P(None, "head"),
    )
    return jax.shard_map(
        on_device,
        mesh=mesh,
        in_specs=placed,
        out_specs=(P(("grp", "tm"), "head"), P("head", ("grp", "tm"))),
        check_vma=False,
    )
```

profile of v0, /device:TPU:0, one launch (start us, length us, event | category | flops | bytes accessed | tf_op | source)
XLA Modules:
  0.0 97.1 jit_solution(13808914991739466856)
XLA Ops:
  0.7 1.4 %fusion.24 = (s32[1]{0:T(128)}, s32[1]{0:T(128)}, s32[1]{0:T(128)}, s32[1]{0:T(128)}) fusion(s32[4]{0:T(128)} %param.14), kind=kLoop, calls=%fused_computation.71 | loop fusion | bytes 32 | tf_op jit(solution)/shard_map/jit(_take)/gather | solution.py:88
  2.1 2.5 %compare_and_fusion.1 = (pred[128]{0:T(512)(128)(4,1)S(1)}, s32[128]{0:T(128)S(1)}, pred[128]{0:T(512)(128)(4,1)S(1)}) fusion(s32[]{:T(128)S(6)} %mul.77, s32[]{:T(128)} %bitcast.4, s32[]{:T(128)} %bitcast.3, s32[]{:T(128)} %bitcast.2, s32[]{:T(128)} %bitcast.1), kind=kLoop, calls=%fused_computation.55 | loop fusion | flops 6912 | bytes 788 | tf_op jit(solution)/shard_map/jit(_take)/and | solution.py:88
  4.6 1.3 %gather_fusion.2 = s32[128,4]{1,0:T(8,128)S(1)} fusion(s32[4,4]{1,0:T(4,128)} %param.13, s32[1024]{0:T(1024)S(1)} %pad_clamp_fusion.2), kind=kCustom, calls=%fused_computation.3 | custom fusion | bytes 4608 | tf_op jit(solution)/shard_map/jit(_take)/gather | solution.py:60
  6.1 0.6 gather_fusion.3
  8.4 0.8 convolution_add_fusion
  9.2 1.6 %copy.27 = bf16[128,4,6,128]{3,0,2,1:T(8,128)(2,1)S(1)} copy(bf16[128,4,6,128]{0,3,2,1:T(8,128)(2,1)} %bitcast.60) | data formatting | bytes 1572864
  11.1 82.1 %while.22 = (s32[]{:T(128)}, bf16[2,128,512]{1,2,0:T(8,128)(2,1)S(1)}, f32[4,6,128]{2,1,0:T(8,128)S(1)}, f32[4,6,128]{2,1,0:T(8,128)S(1)}, f32[4,6,128,128]{3,2,...) while((s32[]{:T(128)}, ...), condition=%wide.region_5.7_spmd.clone, body=%wide.region_2.6_spmd.clone.sunk | while | flops 205697168 | bytes 11474994 | solution.py:82
  11.1 3.0 %collective-permute-start = (bf16[2,128,512]{1,2,0:T(8,128)(2,1)S(1)}, bf16[2,128,512]{1,2,0:T(8,128)(2,1)S(1)}, u32[]{:S(2)}, u32[]{:S(2)}) collective-permute-start(bf16[2,128,512]{1,2,0:T(8,128)(2,1)S(1)} %get-tuple-element.373), channel_id=1, source_target_pairs={{0,2},{2,4},{4,6},{6,8},{8,10},{10,12},{12,14},{14,0},{1,3},{3,5},... | collective-permute-start | bytes 786440 | tf_op jit(solution)/shard_map/while/body/eval_jaxpr/ppermute | solution.py:18
  14.2 0.6 gather_fusion
  14.9 8.6 %collective-permute-done = bf16[2,128,512]{1,2,0:T(8,128)(2,1)S(1)} collective-permute-done((bf16[2,128,512]{1,2,0:T(8,128)(2,1)S(1)}, bf16[2,128,512]{1,2,0:T(8,128)(2,1)S(1)}, u32[]{:S(2)}, u32[]{:S(2)}) %collective-permute-start) | collective-permute-done | bytes 262176 | tf_op jit(solution)/shard_map/while/body/eval_jaxpr/ppermute | solution.py:18
  24.3 1.1 %multiply_add_fusion.5 = f32[4,6,128,128]{3,2,1,0:T(8,128)S(1)} fusion(f32[4,6,128,128]{3,2,1,0:T(8,128)S(1)} %get-tuple-element.376, bf16[128,4,128,1]{0,2,3,1:T(8,128)(2,1)S(1)} %bitcast.57, f32[4,6,128,128]{2,3,1,0:T(8,128)S(1)} %get-tuple-element.355, f32[4,6,128]{2,1,0:T(8,128)S(1)} %get-tuple-element.358, f32[4,6,128]{2,1,0:T(8,128)S(1)} %max.12, ...), kind=kOutput, calls=%fused_computation.6.clone.1 | convolution fusion | flops 102629376 | bytes 4890624 | tf_op jit(solution)/shard_map/while/body/eval_jaxpr/kgqn,nkd->kgqd/dot_general | solution.py:36
  25.6 0.6 gather_fusion
  26.3 9.3 %collective-permute-done = bf16[2,128,512]{1,2,0:T(8,128)(2,1)S(1)} collective-permute-done((bf16[2,128,512]{1,2,0:T(8,128)(2,1)S(1)}, bf16[2,128,512]{1,2,0:T(8,128)(2,1)S(1)}, u32[]{:S(2)}, u32[]{:S(2)}) %collective-permute-start) | collective-permute-done | bytes 262176 | tf_op jit(solution)/shard_map/while/body/eval_jaxpr/ppermute | solution.py:18
  36.5 1.1 %multiply_add_fusion.5 = f32[4,6,128,128]{3,2,1,0:T(8,128)S(1)} fusion(f32[4,6,128,128]{3,2,1,0:T(8,128)S(1)} %get-tuple-element.376, bf16[128,4,128,1]{0,2,3,1:T(8,128)(2,1)S(1)} %bitcast.57, f32[4,6,128,128]{2,3,1,0:T(8,128)S(1)} %get-tuple-element.355, f32[4,6,128]{2,1,0:T(8,128)S(1)} %get-tuple-element.358, f32[4,6,128]{2,1,0:T(8,128)S(1)} %max.12, ...), kind=kOutput, calls=%fused_computation.6.clone.1 | convolution fusion | flops 102629376 | bytes 4890624 | tf_op jit(solution)/shard_map/while/body/eval_jaxpr/kgqn,nkd->kgqd/dot_general | solution.py:36
  37.8 0.6 gather_fusion
  38.5 8.5 %collective-permute-done = bf16[2,128,512]{1,2,0:T(8,128)(2,1)S(1)} collective-permute-done((bf16[2,128,512]{1,2,0:T(8,128)(2,1)S(1)}, bf16[2,128,512]{1,2,0:T(8,128)(2,1)S(1)}, u32[]{:S(2)}, u32[]{:S(2)}) %collective-permute-start) | collective-permute-done | bytes 262176 | tf_op jit(solution)/shard_map/while/body/eval_jaxpr/ppermute | solution.py:18
  47.8 1.1 %multiply_add_fusion.5 = f32[4,6,128,128]{3,2,1,0:T(8,128)S(1)} fusion(f32[4,6,128,128]{3,2,1,0:T(8,128)S(1)} %get-tuple-element.376, bf16[128,4,128,1]{0,2,3,1:T(8,128)(2,1)S(1)} %bitcast.57, f32[4,6,128,128]{2,3,1,0:T(8,128)S(1)} %get-tuple-element.355, f32[4,6,128]{2,1,0:T(8,128)S(1)} %get-tuple-element.358, f32[4,6,128]{2,1,0:T(8,128)S(1)} %max.12, ...), kind=kOutput, calls=%fused_computation.6.clone.1 | convolution fusion | flops 102629376 | bytes 4890624 | tf_op jit(solution)/shard_map/while/body/eval_jaxpr/kgqn,nkd->kgqd/dot_general | solution.py:36
  49.1 0.6 gather_fusion
  49.8 8.2 %collective-permute-done = bf16[2,128,512]{1,2,0:T(8,128)(2,1)S(1)} collective-permute-done((bf16[2,128,512]{1,2,0:T(8,128)(2,1)S(1)}, bf16[2,128,512]{1,2,0:T(8,128)(2,1)S(1)}, u32[]{:S(2)}, u32[]{:S(2)}) %collective-permute-start) | collective-permute-done | bytes 262176 | tf_op jit(solution)/shard_map/while/body/eval_jaxpr/ppermute | solution.py:18
  58.9 1.1 %multiply_add_fusion.5 = f32[4,6,128,128]{3,2,1,0:T(8,128)S(1)} fusion(f32[4,6,128,128]{3,2,1,0:T(8,128)S(1)} %get-tuple-element.376, bf16[128,4,128,1]{0,2,3,1:T(8,128)(2,1)S(1)} %bitcast.57, f32[4,6,128,128]{2,3,1,0:T(8,128)S(1)} %get-tuple-element.355, f32[4,6,128]{2,1,0:T(8,128)S(1)} %get-tuple-element.358, f32[4,6,128]{2,1,0:T(8,128)S(1)} %max.12, ...), kind=kOutput, calls=%fused_computation.6.clone.1 | convolution fusion | flops 102629376 | bytes 4890624 | tf_op jit(solution)/shard_map/while/body/eval_jaxpr/kgqn,nkd->kgqd/dot_general | solution.py:36
  60.1 0.6 gather_fusion
  60.9 8.2 %collective-permute-done = bf16[2,128,512]{1,2,0:T(8,128)(2,1)S(1)} collective-permute-done((bf16[2,128,512]{1,2,0:T(8,128)(2,1)S(1)}, bf16[2,128,512]{1,2,0:T(8,128)(2,1)S(1)}, u32[]{:S(2)}, u32[]{:S(2)}) %collective-permute-start) | collective-permute-done | bytes 262176 | tf_op jit(solution)/shard_map/while/body/eval_jaxpr/ppermute | solution.py:18
  69.9 1.1 %multiply_add_fusion.5 = f32[4,6,128,128]{3,2,1,0:T(8,128)S(1)} fusion(f32[4,6,128,128]{3,2,1,0:T(8,128)S(1)} %get-tuple-element.376, bf16[128,4,128,1]{0,2,3,1:T(8,128)(2,1)S(1)} %bitcast.57, f32[4,6,128,128]{2,3,1,0:T(8,128)S(1)} %get-tuple-element.355, f32[4,6,128]{2,1,0:T(8,128)S(1)} %get-tuple-element.358, f32[4,6,128]{2,1,0:T(8,128)S(1)} %max.12, ...), kind=kOutput, calls=%fused_computation.6.clone.1 | convolution fusion | flops 102629376 | bytes 4890624 | tf_op jit(solution)/shard_map/while/body/eval_jaxpr/kgqn,nkd->kgqd/dot_general | solution.py:36
  71.2 0.6 gather_fusion
  72.0 8.2 %collective-permute-done = bf16[2,128,512]{1,2,0:T(8,128)(2,1)S(1)} collective-permute-done((bf16[2,128,512]{1,2,0:T(8,128)(2,1)S(1)}, bf16[2,128,512]{1,2,0:T(8,128)(2,1)S(1)}, u32[]{:S(2)}, u32[]{:S(2)}) %collective-permute-start) | collective-permute-done | bytes 262176 | tf_op jit(solution)/shard_map/while/body/eval_jaxpr/ppermute | solution.py:18
  81.0 1.1 %multiply_add_fusion.5 = f32[4,6,128,128]{3,2,1,0:T(8,128)S(1)} fusion(f32[4,6,128,128]{3,2,1,0:T(8,128)S(1)} %get-tuple-element.376, bf16[128,4,128,1]{0,2,3,1:T(8,128)(2,1)S(1)} %bitcast.57, f32[4,6,128,128]{2,3,1,0:T(8,128)S(1)} %get-tuple-element.355, f32[4,6,128]{2,1,0:T(8,128)S(1)} %get-tuple-element.358, f32[4,6,128]{2,1,0:T(8,128)S(1)} %max.12, ...), kind=kOutput, calls=%fused_computation.6.clone.1 | convolution fusion | flops 102629376 | bytes 4890624 | tf_op jit(solution)/shard_map/while/body/eval_jaxpr/kgqn,nkd->kgqd/dot_general | solution.py:36
  82.3 0.6 gather_fusion
  83.0 8.2 %collective-permute-done = bf16[2,128,512]{1,2,0:T(8,128)(2,1)S(1)} collective-permute-done((bf16[2,128,512]{1,2,0:T(8,128)(2,1)S(1)}, bf16[2,128,512]{1,2,0:T(8,128)(2,1)S(1)}, u32[]{:S(2)}, u32[]{:S(2)}) %collective-permute-start) | collective-permute-done | bytes 262176 | tf_op jit(solution)/shard_map/while/body/eval_jaxpr/ppermute | solution.py:18
  92.1 1.1 %multiply_add_fusion.5 = f32[4,6,128,128]{3,2,1,0:T(8,128)S(1)} fusion(f32[4,6,128,128]{3,2,1,0:T(8,128)S(1)} %get-tuple-element.376, bf16[128,4,128,1]{0,2,3,1:T(8,128)(2,1)S(1)} %bitcast.57, f32[4,6,128,128]{2,3,1,0:T(8,128)S(1)} %get-tuple-element.355, f32[4,6,128]{2,1,0:T(8,128)S(1)} %get-tuple-element.358, f32[4,6,128]{2,1,0:T(8,128)S(1)} %max.12, ...), kind=kOutput, calls=%fused_computation.6.clone.1 | convolution fusion | flops 102629376 | bytes 4890624 | tf_op jit(solution)/shard_map/while/body/eval_jaxpr/kgqn,nkd->kgqd/dot_general | solution.py:36
  93.2 0.6 reshape.138
  95.0 1.0 %gather_fusion.1 = f32[128,3072]{1,0:T(8,128)S(1)} fusion(f32[4,3072]{1,0:T(4,128)S(1)} %copy-done, s32[1024]{0:T(1024)S(1)} %pad_clamp_fusion.3), kind=kCustom, calls=%fused_computation.2 | custom fusion | bytes 3146240 | tf_op jit(solution)/shard_map/jit(_take)/gather | solution.py:88
  96.0 1.1 %multiply_convert_fusion = bf16[128,3072]{1,0:T(8,128)(2,1)} fusion(f32[128,3072]{1,0:T(8,128)S(1)} %copy.29, f32[128,3072]{1,0:T(8,128)S(1)} %gather_fusion.1, pred[128]{0:T(512)(128)(4,1)S(1)} %get-tuple-element.283), kind=kLoop, calls=%fused_computation.27 | loop fusion | flops 1179648 | bytes 3932288 | tf_op jit(solution)/shard_map/convert_element_type | solution.py:89
  (118 shorter events, 10.0 us)
Async XLA Ops:
  0.6 94.4 %copy-start = (f32[4,3072]{1,0:T(4,128)S(1)}, f32[4,3072]{1,0:T(4,128)}, u32[]{:S(2)}) copy-start(f32[4,3072]{1,0:T(4,128)} %param.15) | copy-start | bytes 147460
  0.6 6.2 %copy-start.2 = (bf16[128,3072]{1,0:T(8,128)(2,1)S(1)}, bf16[128,3072]{1,0:T(8,128)(2,1)}, u32[]{:S(2)}) copy-start(bf16[128,3072]{1,0:T(8,128)(2,1)} %param.10) | copy-start | bytes 2359300
  0.7 6.6 %copy-start.3 = (bf16[128,512]{1,0:T(8,128)(2,1)S(1)}, bf16[128,512]{1,0:T(8,128)(2,1)}, u32[]{:S(2)}) copy-start(bf16[128,512]{1,0:T(8,128)(2,1)} %param.11) | copy-start | bytes 393220
  7.3 0.9 copy-start.1
  7.3 1.1 %copy-start.4 = (bf16[128,512]{1,0:T(8,128)(2,1)S(1)}, bf16[128,512]{1,0:T(8,128)(2,1)}, u32[]{:S(2)}) copy-start(bf16[128,512]{1,0:T(8,128)(2,1)} %param.12) | copy-start | bytes 393220
  9.2 1.7 %copy-start.5 = (bf16[128,512]{1,0:T(8,128)(2,1)S(1)}, bf16[128,512]{1,0:T(8,128)(2,1)}, u32[]{:S(2)}) copy-start(bf16[128,512]{1,0:T(8,128)(2,1)} %param.12) | copy-start | bytes 393220
  11.1 12.4 %collective-permute-start = (bf16[2,128,512]{1,2,0:T(8,128)(2,1)S(1)}, bf16[2,128,512]{1,2,0:T(8,128)(2,1)S(1)}, u32[]{:S(2)}, u32[]{:S(2)}) collective-permute-start(bf16[2,128,512]{1,2,0:T(8,128)(2,1)S(1)} %get-tuple-element.373), channel_id=1, source_target_pairs={{0,2},{2,4},{4,6},{6,8},{8,10},{10,12},{12,14},{14,0},{1,3},{3,5},... | collective-permute-start | bytes 786440 | tf_op jit(solution)/shard_map/while/body/eval_jaxpr/ppermute | solution.py:18
  25.5 10.2 %collective-permute-start = (bf16[2,128,512]{1,2,0:T(8,128)(2,1)S(1)}, bf16[2,128,512]{1,2,0:T(8,128)(2,1)S(1)}, u32[]{:S(2)}, u32[]{:S(2)}) collective-permute-start(bf16[2,128,512]{1,2,0:T(8,128)(2,1)S(1)} %get-tuple-element.373), channel_id=1, source_target_pairs={{0,2},{2,4},{4,6},{6,8},{8,10},{10,12},{12,14},{14,0},{1,3},{3,5},... | collective-permute-start | bytes 786440 | tf_op jit(solution)/shard_map/while/body/eval_jaxpr/ppermute | solution.py:18
  37.6 9.4 %collective-permute-start = (bf16[2,128,512]{1,2,0:T(8,128)(2,1)S(1)}, bf16[2,128,512]{1,2,0:T(8,128)(2,1)S(1)}, u32[]{:S(2)}, u32[]{:S(2)}) collective-permute-start(bf16[2,128,512]{1,2,0:T(8,128)(2,1)S(1)} %get-tuple-element.373), channel_id=1, source_target_pairs={{0,2},{2,4},{4,6},{6,8},{8,10},{10,12},{12,14},{14,0},{1,3},{3,5},... | collective-permute-start | bytes 786440 | tf_op jit(solution)/shard_map/while/body/eval_jaxpr/ppermute | solution.py:18
  48.9 9.1 %collective-permute-start = (bf16[2,128,512]{1,2,0:T(8,128)(2,1)S(1)}, bf16[2,128,512]{1,2,0:T(8,128)(2,1)S(1)}, u32[]{:S(2)}, u32[]{:S(2)}) collective-permute-start(bf16[2,128,512]{1,2,0:T(8,128)(2,1)S(1)} %get-tuple-element.373), channel_id=1, source_target_pairs={{0,2},{2,4},{4,6},{6,8},{8,10},{10,12},{12,14},{14,0},{1,3},{3,5},... | collective-permute-start | bytes 786440 | tf_op jit(solution)/shard_map/while/body/eval_jaxpr/ppermute | solution.py:18
  60.0 9.1 %collective-permute-start = (bf16[2,128,512]{1,2,0:T(8,128)(2,1)S(1)}, bf16[2,128,512]{1,2,0:T(8,128)(2,1)S(1)}, u32[]{:S(2)}, u32[]{:S(2)}) collective-permute-start(bf16[2,128,512]{1,2,0:T(8,128)(2,1)S(1)} %get-tuple-element.373), channel_id=1, source_target_pairs={{0,2},{2,4},{4,6},{6,8},{8,10},{10,12},{12,14},{14,0},{1,3},{3,5},... | collective-permute-start | bytes 786440 | tf_op jit(solution)/shard_map/while/body/eval_jaxpr/ppermute | solution.py:18
  71.1 9.1 %collective-permute-start = (bf16[2,128,512]{1,2,0:T(8,128)(2,1)S(1)}, bf16[2,128,512]{1,2,0:T(8,128)(2,1)S(1)}, u32[]{:S(2)}, u32[]{:S(2)}) collective-permute-start(bf16[2,128,512]{1,2,0:T(8,128)(2,1)S(1)} %get-tuple-element.373), channel_id=1, source_target_pairs={{0,2},{2,4},{4,6},{6,8},{8,10},{10,12},{12,14},{14,0},{1,3},{3,5},... | collective-permute-start | bytes 786440 | tf_op jit(solution)/shard_map/while/body/eval_jaxpr/ppermute | solution.py:18
  82.2 9.1 %collective-permute-start = (bf16[2,128,512]{1,2,0:T(8,128)(2,1)S(1)}, bf16[2,128,512]{1,2,0:T(8,128)(2,1)S(1)}, u32[]{:S(2)}, u32[]{:S(2)}) collective-permute-start(bf16[2,128,512]{1,2,0:T(8,128)(2,1)S(1)} %get-tuple-element.373), channel_id=1, source_target_pairs={{0,2},{2,4},{4,6},{6,8},{8,10},{10,12},{12,14},{14,0},{1,3},{3,5},... | collective-permute-start | bytes 786440 | tf_op jit(solution)/shard_map/while/body/eval_jaxpr/ppermute | solution.py:18
where the time goes:
time: 97.4 us; the launch traced here: 97.1 us
  waiting for transfers between devices  59.3 us (61%)
  local copies, waits for them, and re-layouts  13.4 us (14%)
  matrix products  11.9 us (12%)
  other arithmetic  7.4 us (8%)
  starting transfers between devices  3.4 us (3%)
    ppermute x7, waiting for transfers between devices, from_behind(): return lax.ppermute(value, axis, pairs)  59.3 us
    dot_general x8, matrix products, attend_block(): jnp.einsum('kgqn,nkd->kgqd', weight.astype(jnp.bfloat16), values_three, p...  8.37 us
    gather x7, local copies, waits for them, and re-layouts, hop(): jnp.take(row_mask, key_spans, axis=1) > 0  4.51 us
    dot_general x8, matrix products, attend_block(): jnp.einsum('qkgd,nkd->kgqn', grouped, keys_three, preferred_element_type=...  3.52 us
    ppermute x7, starting transfers between devices, from_behind(): return lax.ppermute(value, axis, pairs)  3.4 us
    unnamed x16, local copies, waits for them, and re-layouts  2.59 us
    and x1, other arithmetic, on_device(): gate_rows = jnp.take(section_gate, jnp.take(section, query_spans), axis=0)  2.49 us
    gather x2, local copies, waits for them, and re-layouts, on_device(): gate_rows = jnp.take(section_gate, jnp.take(section, query_spans), axis=0)  2.38 us
  transfers between devices with their start and end apart: 7, of which 7 were waited for; matrix products, arithmetic and copies ran while one was open for 6% of the time, Pallas kernels for 0%

commit v1 on v0

v1 whole, which is shorter than its diff:
```python
import functools
import math

import jax
import jax.numpy as jnp
from jax import lax
from jax.experimental import pallas as pl
from jax.experimental.pallas import tpu as pltpu
from jax.sharding import PartitionSpec as P

HEAD_SIZE = 128
CH = 256
MESH = pl.DeviceIdType.MESH
LOG2E = 1.4426950408889634
LN2 = 0.6931471805599453
FAR = 1e30


def kernel(
    count, chunks, q_hbm, k_hbm, v_hbm, mask_ref, sec_ref, gate_ref, out_ref, lt_ref,
    qbuf, kbuf, vbuf, top_s, tot_s, acc_s, ltm_s, gate_s, qsem, ksem, vsem,
    krecv, vrecv, kz, vz, ky, vy,
):
    q_heads, rows = qbuf.shape[0], qbuf.shape[1]
    kv_heads = kbuf.shape[1]
    group = q_heads // kv_heads
    per = kv_heads // chunks
    pairs = count // 2
    factor = LOG2E / math.sqrt(HEAD_SIZE)

    me = lax.axis_index("tm")
    pair = me // 2
    side = me % 2
    partner = me + 1 - 2 * side
    has_prev = pair > 0
    has_next = pair < pairs - 1

    def head_copy(src, dst, sem, head):
        return pltpu.make_async_copy(
            src.at[:, pl.ds(head * HEAD_SIZE, HEAD_SIZE)], dst, sem
        )

    own_k = [head_copy(k_hbm, kbuf.at[me, h], ksem.at[h], h) for h in range(kv_heads)]
    own_v = [head_copy(v_hbm, vbuf.at[me, h], vsem.at[h], h) for h in range(kv_heads)]
    own_q = [head_copy(q_hbm, qbuf.at[h], qsem.at[h], h) for h in range(q_heads)]
    for copy in own_k + own_v:
        copy.start()

    barrier = pltpu.get_barrier_semaphore()
    pl.semaphore_signal(barrier, inc=1, device_id={"tm": partner}, device_id_type=MESH)

    @pl.when(has_next)
    def _():
        pl.semaphore_signal(barrier, inc=1, device_id={"tm": me + 2}, device_id_type=MESH)

    @pl.when(has_prev)
    def _():
        pl.semaphore_signal(barrier, inc=1, device_id={"tm": me - 2}, device_id_type=MESH)

    for copy in own_q:
        copy.start()
    pl.semaphore_wait(
        barrier, 1 + has_next.astype(jnp.int32) + has_prev.astype(jnp.int32)
    )

    def send(buf, send_sem, recv_sem, slot, c, target):
        piece = buf.at[slot, pl.ds(c * per, per)]
        return pltpu.make_async_remote_copy(
            src_ref=piece,
            dst_ref=piece,
            send_sem=send_sem.at[slot, c],
            recv_sem=recv_sem.at[slot, c],
            device_id={"tm": target},
            device_id_type=MESH,
        )

    def k_on(slot, c):
        return send(kbuf, kz, krecv, slot, c, me + 2)

    def v_on(slot, c):
        return send(vbuf, vz, vrecv, slot, c, me + 2)

    def k_over(slot, c):
        return send(kbuf, ky, krecv, slot, c, partner)

    def v_over(slot, c):
        return send(vbuf, vy, vrecv, slot, c, partner)

    for c in range(chunks):
        for h in range(c * per, (c + 1) * per):
            own_k[h].wait()

        @pl.when(has_next)
        def _():
            k_on(me, c).start()

        k_over(me, c).start()
        for h in range(c * per, (c + 1) * per):
            own_v[h].wait()

        @pl.when(has_next)
        def _():
            v_on(me, c).start()

        v_over(me, c).start()

    def visit(slots, first, last):
        allowed = [mask_ref[pair, slot // 2] > 0 for slot in slots]

        def one(head, carry):
            keys = jnp.concatenate([kbuf[slot, head] for slot in slots], axis=0)
            vals = jnp.concatenate([vbuf[slot, head] for slot in slots], axis=0)
            for g in range(group):
                j = head * group + g
                score = factor * lax.dot_general(
                    qbuf[j], keys, (((1,), (1,)), ((), ())),
                    preferred_element_type=jnp.float32,
                )
                parts = [score[:, i * rows:(i + 1) * rows] for i in range(len(slots))]
                tops = [
                    jnp.where(ok, jnp.max(part, axis=1, keepdims=True), -FAR)
                    for ok, part in zip(allowed, parts)
                ]
                top = functools.reduce(jnp.maximum, tops)
                if not first:
                    before = top_s[j]
                    top = jnp.maximum(before, top)
                top = jnp.broadcast_to(top, (rows, HEAD_SIZE))
                weights = [
                    jnp.exp2(part - jnp.where(ok, top, FAR))
                    for ok, part in zip(allowed, parts)
                ]
                total = functools.reduce(jnp.add, weights)
                weight = jnp.concatenate(
                    [w.astype(jnp.bfloat16) for w in weights], axis=1
                )
                acc = jnp.dot(weight, vals, preferred_element_type=jnp.float32)
                if not first:
                    fade = jnp.exp2(before - top)
                    total = total + tot_s[j] * fade
                    acc = acc + acc_s[j] * fade
                if last:
                    full = jnp.sum(total, axis=1, keepdims=True)
                    cols = pl.ds(pl.multiple_of(j * HEAD_SIZE, HEAD_SIZE), HEAD_SIZE)
                    gate = gate_s[:, cols]
                    out_ref[:, cols] = (gate * (acc / full)).astype(out_ref.dtype)
                    log_total = top * LN2 + jnp.log(full)
                    lane = lax.broadcasted_iota(jnp.int32, (rows, HEAD_SIZE), 1)
                    ltm_s[...] = jnp.where(lane == j, log_total, ltm_s[...])
                else:
                    top_s[j] = top
                    tot_s[j] = total
                    acc_s[j] = acc
            return carry

        lax.fori_loop(0, kv_heads, one, 0)

    for copy in own_q:
        copy.wait()
    visit([me], True, False)
    gate_row = gate_ref[pl.ds(0, 1), :]
    for i in range(1, gate_ref.shape[0]):
        gate_row = jnp.where(sec_ref[pair] == i, gate_ref[pl.ds(i, 1), :], gate_row)
    gate_s[...] = gate_row
    ltm_s[...] = jnp.zeros_like(ltm_s)

    def step(i, carry):
        behind = me - 2 * i
        across = partner - 2 * (i - 1)
        for c in range(chunks):
            k_on(behind, c).wait_recv()

            @pl.when(has_next)
            def _():
                k_on(behind, c).start()

            k_over(behind, c).start()
            v_on(behind, c).wait_recv()

            @pl.when(has_next)
            def _():
                v_on(behind, c).start()

            @pl.when(behind >= 2)
            def _():
                v_over(behind, c).start()

        for c in range(chunks):
            k_over(across, c).wait_recv()
            v_over(across, c).wait_recv()
        visit([behind, across], False, False)
        return carry

    lax.fori_loop(1, pair + 1, step, 0)

    far = 1 - side
    for c in range(chunks):
        v_on(far, c).wait_recv()

        @pl.when(has_next)
        def _():
            v_on(far, c).start()

    for c in range(chunks):
        k_over(far, c).wait_recv()
    visit([far], False, True)
    lt_ref[...] = jnp.transpose(ltm_s[...])[:q_heads]

    def settle(i, carry):
        slot = me - 2 * i
        for c in range(chunks):

            @pl.when(has_next)
            def _():
                k_on(slot, c).wait_send()
                v_on(slot, c).wait_send()

            k_over(slot, c).wait_send()

            @pl.when((slot >= 2) | (i == 0))
            def _():
                v_over(slot, c).wait_send()

        return carry

    lax.fori_loop(0, pair + 1, settle, 0)

    @pl.when(has_next)
    def _():
        for c in range(chunks):
            v_on(far, c).wait_send()


def solution(mesh):
    count = mesh.shape["tm"]

    def on_device(queries, keys, values, span_mask, section, section_gate):
        rows = queries.shape[0]
        q_heads = queries.shape[1] // HEAD_SIZE
        kv_heads = keys.shape[1] // HEAD_SIZE
        assert CH == 2 * rows and count % 2 == 0
        chunks = 2 if kv_heads % 2 == 0 else 1
        any_spec = pl.BlockSpec(memory_space=pl.ANY)
        smem = pl.BlockSpec(memory_space=pltpu.SMEM)
        vmem = pl.BlockSpec(memory_space=pltpu.VMEM)
        dma = pltpu.SemaphoreType.DMA
        state = pltpu.VMEM((q_heads, rows, HEAD_SIZE), jnp.float32)
        held = pltpu.VMEM((count, kv_heads, rows, HEAD_SIZE), jnp.bfloat16)
        return pl.pallas_call(
            functools.partial(kernel, count, chunks),
            out_shape=(
                jax.ShapeDtypeStruct(queries.shape, jnp.bfloat16),
                jax.ShapeDtypeStruct((q_heads, rows), jnp.float32),
            ),
            in_specs=[any_spec] * 3 + [smem, smem, vmem],
            out_specs=(vmem, vmem),
            scratch_shapes=[
                pltpu.VMEM((q_heads, rows, HEAD_SIZE), jnp.bfloat16),
                held, held, state, state, state,
                pltpu.VMEM((rows, HEAD_SIZE), jnp.float32),
                pltpu.VMEM((1, queries.shape[1]), jnp.float32),
                dma((q_heads,)), dma((kv_heads,)), dma((kv_heads,)),
            ] + [dma((count, chunks))] * 6,
            compiler_params=pltpu.CompilerParams(
                collective_id=0, has_side_effects=True, vmem_limit_bytes=40 * 2**20
            ),
            name="span_attention",
        )(queries, keys, values, span_mask, section, section_gate)

    placed = (
        P(("grp", "tm"), "head"),
        P(("grp", "tm"), "head"),
        P(("grp", "tm"), "head"),
        P("grp", None),
        P("grp"),
        P(None, "head"),
    )
    return jax.shard_map(
        on_device,
        mesh=mesh,
        in_specs=placed,
        out_specs=(P(("grp", "tm"), "head"), P("head", ("grp", "tm"))),
        check_vma=False,
    )
```

time: 97.4 us -> 40 us (0.41)
  the two profiles are of different devices: /device:TPU:0 before, /device:TPU:24 now
where the time goes in v1:
time: 40 us; the launch traced here: 39.7 us
  Pallas kernels  32.5 us (81%)
  local copies, waits for them, and re-layouts  6.55 us (16%)
  between operations  0.65 us (2%)
    pallas_call x1, Pallas kernels, on_device(): pl.pallas_call(functools.partial(kernel, count, chunks), out_shape=(jax.S...  32.5 us
    unnamed x14, local copies, waits for them, and re-layouts  6.55 us

profile of v1, /device:TPU:24, one launch (start us, length us, event | category | flops | bytes accessed | tf_op | source)
XLA Modules:
  0.0 39.7 jit_solution(16668933225368495700)
XLA Ops:
  0.6 0.0 copy-start
  0.6 1.1 %copy-done = bf16[128,3072]{1,0:T(8,128)(2,1)S(1)} copy-done((bf16[128,3072]{1,0:T(8,128)(2,1)S(1)}, bf16[128,3072]{1,0:T(8,128)(2,1)}, u32[]{:S(2)}) %copy-start) | copy-done | bytes 786456
  1.8 0.0 copy-start.1
  1.8 0.9 %copy-done.1 = bf16[128,512]{1,0:T(8,128)(2,1)S(1)} copy-done((bf16[128,512]{1,0:T(8,128)(2,1)S(1)}, bf16[128,512]{1,0:T(8,128)(2,1)}, u32[]{:S(2)}) %copy-start.1) | copy-done | bytes 131096
  2.7 0.0 copy-start.2
  2.7 0.9 %copy-done.2 = bf16[128,512]{1,0:T(8,128)(2,1)S(1)} copy-done((bf16[128,512]{1,0:T(8,128)(2,1)S(1)}, bf16[128,512]{1,0:T(8,128)(2,1)}, u32[]{:S(2)}) %copy-start.2) | copy-done | bytes 131096
  3.6 0.0 copy-start.3
  3.6 0.8 %copy-done.3 = f32[4,3072]{1,0:T(4,128)S(1)} copy-done((f32[4,3072]{1,0:T(4,128)S(1)}, f32[4,3072]{1,0:T(4,128)}, u32[]{:S(2)}) %copy-start.3) | copy-done | bytes 49176
  4.4 0.0 copy-start.4
  4.4 0.7 %copy-done.4 = s32[4,4]{1,0:T(4,128)S(1)} copy-done((s32[4,4]{1,0:T(4,128)S(1)}, s32[4,4]{1,0:T(4,128)}, u32[]{:S(2)}) %copy-start.4) | copy-done | bytes 88
  5.1 0.0 copy-start.5
  5.1 0.7 %copy-done.5 = s32[4]{0:T(128)S(1)} copy-done((s32[4]{0:T(128)S(1)}, s32[4]{0:T(128)}, u32[]{:S(2)}) %copy-start.5) | copy-done | bytes 40
  5.7 32.5 %span_attention.1 = (bf16[128,3072]{1,0:T(8,128)(2,1)S(1)}, f32[24,128]{1,0:T(8,128)S(1)}) custom-call(bf16[128,3072]{1,0:T(8,128)(2,1)S(1)} %copy-done, bf16[128,512]{1,0:T(8,128)(2,1)S(1)} %copy-done.1, bf16[128,512]{1,0:T(8,128)(2,1)S(1)} %copy-done.2, s32[4,4]{1,0:T(4,128)S(1)} %copy-done.4, s32[4]{0:T(128)S(1)} %copy-done.5, f32[4,3072]{1,0:T(4,128)S(1)} %copy-done.3), custom_call_target="tpu_custom_call" | custom-call | tf_op jit(solution)/shard_map/span_attention/pallas_call | solution.py:249
  38.2 0.9 %copy.10 = bf16[128,3072]{1,0:T(8,128)(2,1)} copy(bf16[128,3072]{1,0:T(8,128)(2,1)S(1)} %get-tuple-element.4) | data formatting | bytes 1572864
  39.1 0.6 %copy.11 = f32[24,128]{1,0:T(8,128)} copy(f32[24,128]{1,0:T(8,128)S(1)} %get-tuple-element.5) | data formatting | bytes 24576
Async XLA Ops:
  0.6 1.1 %copy-start = (bf16[128,3072]{1,0:T(8,128)(2,1)S(1)}, bf16[128,3072]{1,0:T(8,128)(2,1)}, u32[]{:S(2)}) copy-start(bf16[128,3072]{1,0:T(8,128)(2,1)} %q_hbm.1) | copy-start | bytes 2359300
  1.8 0.9 %copy-start.1 = (bf16[128,512]{1,0:T(8,128)(2,1)S(1)}, bf16[128,512]{1,0:T(8,128)(2,1)}, u32[]{:S(2)}) copy-start(bf16[128,512]{1,0:T(8,128)(2,1)} %k_hbm.1) | copy-start | bytes 393220
  2.7 0.9 %copy-start.2 = (bf16[128,512]{1,0:T(8,128)(2,1)S(1)}, bf16[128,512]{1,0:T(8,128)(2,1)}, u32[]{:S(2)}) copy-start(bf16[128,512]{1,0:T(8,128)(2,1)} %v_hbm.1) | copy-start | bytes 393220
  3.6 0.8 %copy-start.3 = (f32[4,3072]{1,0:T(4,128)S(1)}, f32[4,3072]{1,0:T(4,128)}, u32[]{:S(2)}) copy-start(f32[4,3072]{1,0:T(4,128)} %gate_ref.1) | copy-start | bytes 147460
  4.4 0.7 %copy-start.4 = (s32[4,4]{1,0:T(4,128)S(1)}, s32[4,4]{1,0:T(4,128)}, u32[]{:S(2)}) copy-start(s32[4,4]{1,0:T(4,128)} %mask_ref.1) | copy-start | bytes 196
  5.1 0.7 %copy-start.5 = (s32[4]{0:T(128)S(1)}, s32[4]{0:T(128)}, u32[]{:S(2)}) copy-start(s32[4]{0:T(128)} %sec_ref.1) | copy-start | bytes 52

commit v2 on v1

--- a/solution.py
+++ b/solution.py
@@ -17,8 +17,8 @@
 
 
 def kernel(
-    count, chunks, q_hbm, k_hbm, v_hbm, mask_ref, sec_ref, gate_ref, out_ref, lt_ref,
-    qbuf, kbuf, vbuf, top_s, tot_s, acc_s, ltm_s, gate_s, qsem, ksem, vsem,
+    count, chunks, q_hbm, k_hbm, v_hbm, mask_hbm, sec_hbm, gate_hbm, out_ref, lt_ref,
+    qbuf, kbuf, vbuf, top_s, tot_s, acc_s, ltm_s, gate_s, mask_ref, sec_ref, gate_ref, small, qsem, ksem, vsem,
     krecv, vrecv, kz, vz, ky, vy,
 ):
     q_heads, rows = qbuf.shape[0], qbuf.shape[1]
@@ -26,6 +26,7 @@
     group = q_heads // kv_heads
     per = kv_heads // chunks
     pairs = count // 2
+    tile = group
     factor = LOG2E / math.sqrt(HEAD_SIZE)
 
     me = lax.axis_index("tm")
@@ -57,7 +58,12 @@
     def _():
         pl.semaphore_signal(barrier, inc=1, device_id={"tm": me - 2}, device_id_type=MESH)
 
-    for copy in own_q:
+    own_small = [
+        pltpu.make_async_copy(mask_hbm, mask_ref, small.at[0]),
+        pltpu.make_async_copy(sec_hbm, sec_ref, small.at[1]),
+        pltpu.make_async_copy(gate_hbm, gate_ref, small.at[2]),
+    ]
+    for copy in own_q + own_small:
         copy.start()
     pl.semaphore_wait(
         barrier, 1 + has_next.astype(jnp.int32) + has_prev.astype(jnp.int32)
@@ -104,60 +110,82 @@
 
         v_over(me, c).start()
 
-    def visit(slots, first, last):
+    def visit(slots, head, first, last):
         allowed = [mask_ref[pair, slot // 2] > 0 for slot in slots]
-
-        def one(head, carry):
-            keys = jnp.concatenate([kbuf[slot, head] for slot in slots], axis=0)
-            vals = jnp.concatenate([vbuf[slot, head] for slot in slots], axis=0)
-            for g in range(group):
-                j = head * group + g
-                score = factor * lax.dot_general(
-                    qbuf[j], keys, (((1,), (1,)), ((), ())),
-                    preferred_element_type=jnp.float32,
-                )
-                parts = [score[:, i * rows:(i + 1) * rows] for i in range(len(slots))]
-                tops = [
-                    jnp.where(ok, jnp.max(part, axis=1, keepdims=True), -FAR)
-                    for ok, part in zip(allowed, parts)
-                ]
-                top = functools.reduce(jnp.maximum, tops)
-                if not first:
-                    before = top_s[j]
-                    top = jnp.maximum(before, top)
-                top = jnp.broadcast_to(top, (rows, HEAD_SIZE))
-                weights = [
-                    jnp.exp2(part - jnp.where(ok, top, FAR))
-                    for ok, part in zip(allowed, parts)
-                ]
-                total = functools.reduce(jnp.add, weights)
-                weight = jnp.concatenate(
-                    [w.astype(jnp.bfloat16) for w in weights], axis=1
-                )
-                acc = jnp.dot(weight, vals, preferred_element_type=jnp.float32)
-                if not first:
-                    fade = jnp.exp2(before - top)
-                    total = total + tot_s[j] * fade
-                    acc = acc + acc_s[j] * fade
-                if last:
-                    full = jnp.sum(total, axis=1, keepdims=True)
-                    cols = pl.ds(pl.multiple_of(j * HEAD_SIZE, HEAD_SIZE), HEAD_SIZE)
-                    gate = gate_s[:, cols]
-                    out_ref[:, cols] = (gate * (acc / full)).astype(out_ref.dtype)
-                    log_total = top * LN2 + jnp.log(full)
-                    lane = lax.broadcasted_iota(jnp.int32, (rows, HEAD_SIZE), 1)
-                    ltm_s[...] = jnp.where(lane == j, log_total, ltm_s[...])
-                else:
-                    top_s[j] = top
-                    tot_s[j] = total
-                    acc_s[j] = acc
-            return carry
-
-        lax.fori_loop(0, kv_heads, one, 0)
+        keys = jnp.concatenate([kbuf[slot, head] for slot in slots], axis=0)
+        vals = jnp.concatenate([vbuf[slot, head] for slot in slots], axis=0)
+        base = head * group
+        tiles = range(0, group, tile)
+        tall = tile * rows
+
+        def held(ref, g):
+            return ref[pl.ds(base + g, tile)].reshape(tall, HEAD_SIZE)
+
+        def keep(ref, g, value):
+            ref[pl.ds(base + g, tile)] = value.reshape(tile, rows, HEAD_SIZE)
+
+        if not first:
+            before = [held(top_s, g) for g in tiles]
+            tot_old = [held(tot_s, g) for g in tiles]
+            acc_old = [held(acc_s, g) for g in tiles]
+        done = []
+        for n, g in enumerate(tiles):
+            score = factor * lax.dot_general(
+                held(qbuf, g), keys, (((1,), (1,)), ((), ())),
+                preferred_element_type=jnp.float32,
+            )
+            parts = [score[:, i * rows:(i + 1) * rows] for i in range(len(slots))]
+            tops = [
+                jnp.where(ok, jnp.max(part, axis=1, keepdims=True), -FAR)
+                for ok, part in zip(allowed, parts)
+            ]
+            top = functools.reduce(jnp.maximum, tops)
+            if not first:
+                top = jnp.maximum(before[n], top)
+            top = jnp.broadcast_to(top, (tall, HEAD_SIZE))
+            weights = [
+                jnp.exp2(part - jnp.where(ok, top, FAR))
+                for ok, part in zip(allowed, parts)
+            ]
+            total = functools.reduce(jnp.add, weights)
+            weight = jnp.concatenate([w.astype(jnp.bfloat16) for w in weights], axis=1)
+            acc = jnp.dot(weight, vals, preferred_element_type=jnp.float32)
+            if not first:
+                fade = jnp.exp2(before[n] - top)
+                total = total + tot_old[n] * fade
+                acc = acc + acc_old[n] * fade
+            done.append((top, total, acc))
+        if not last:
+            for n, g in enumerate(tiles):
+                keep(top_s, g, done[n][0])
+                keep(tot_s, g, done[n][1])
+                keep(acc_s, g, done[n][2])
+            return
+        lane = lax.broadcasted_iota(jnp.int32, (rows, HEAD_SIZE), 1)
+        sums = ltm_s[...]
+        for n, g in enumerate(tiles):
+            top, total, acc = done[n]
+            full = jnp.sum(total, axis=1, keepdims=True)
+            attended = acc / full
+            log_total = top * LN2 + jnp.log(full)
+            for t in range(tile):
+                j = base + g + t
+                cut = slice(t * rows, (t + 1) * rows)
+                cols = pl.ds(pl.multiple_of(j * HEAD_SIZE, HEAD_SIZE), HEAD_SIZE)
+                out_ref[:, cols] = (gate_s[:, cols] * attended[cut]).astype(out_ref.dtype)
+                sums = jnp.where(lane == j, log_total[cut], sums)
+        ltm_s[...] = sums
 
     for copy in own_q:
         copy.wait()
-    visit([me], True, False)
+    for copy in own_small:
+        copy.wait()
+
+    def own(head, carry):
+        visit([me], head, True, False)
+        return carry
+
+    lax.fori_loop(0, kv_heads, own, 0)
     gate_row = gate_ref[pl.ds(0, 1), :]
     for i in range(1, gate_ref.shape[0]):
         gate_row = jnp.where(sec_ref[pair] == i, gate_ref[pl.ds(i, 1), :], gate_row)
@@ -167,7 +195,8 @@
     def step(i, carry):
         behind = me - 2 * i
         across = partner - 2 * (i - 1)
-        for c in range(chunks):
+
+        def at_head(c, inner):
             k_on(behind, c).wait_recv()
 
             @pl.when(has_next)
@@ -185,25 +214,29 @@
             def _():
                 v_over(behind, c).start()
 
-        for c in range(chunks):
             k_over(across, c).wait_recv()
             v_over(across, c).wait_recv()
-        visit([behind, across], False, False)
-        return carry
+            visit([behind, across], c, False, False)
+            return inner
+
+        return lax.fori_loop(0, kv_heads, at_head, carry)
 
     lax.fori_loop(1, pair + 1, step, 0)
 
     far = 1 - side
-    for c in range(chunks):
+
+    def end(c, carry):
         v_on(far, c).wait_recv()
 
         @pl.when(has_next)
         def _():
             v_on(far, c).start()
 
-    for c in range(chunks):
         k_over(far, c).wait_recv()
-    visit([far], False, True)
+        visit([far], c, False, True)
+        return carry
+
+    lax.fori_loop(0, kv_heads, end, 0)
     lt_ref[...] = jnp.transpose(ltm_s[...])[:q_heads]
 
     def settle(i, carry):
@@ -239,9 +272,7 @@
         q_heads = queries.shape[1] // HEAD_SIZE
         kv_heads = keys.shape[1] // HEAD_SIZE
         assert CH == 2 * rows and count % 2 == 0
-        chunks = 2 if kv_heads % 2 == 0 else 1
-        any_spec = pl.BlockSpec(memory_space=pl.ANY)
-        smem = pl.BlockSpec(memory_space=pltpu.SMEM)
+        chunks = kv_heads
         vmem = pl.BlockSpec(memory_space=pltpu.VMEM)
         dma = pltpu.SemaphoreType.DMA
         state = pltpu.VMEM((q_heads, rows, HEAD_SIZE), jnp.float32)
@@ -249,20 +280,23 @@
         return pl.pallas_call(
             functools.partial(kernel, count, chunks),
             out_shape=(
-                jax.ShapeDtypeStruct(queries.shape, jnp.bfloat16),
-                jax.ShapeDtypeStruct((q_heads, rows), jnp.float32),
+                pltpu.VMEM(queries.shape, jnp.bfloat16),
+                pltpu.VMEM((q_heads, rows), jnp.float32),
             ),
-            in_specs=[any_spec] * 3 + [smem, smem, vmem],
+            in_specs=[pl.BlockSpec(memory_space=pltpu.HBM)] * 6,
             out_specs=(vmem, vmem),
             scratch_shapes=[
                 pltpu.VMEM((q_heads, rows, HEAD_SIZE), jnp.bfloat16),
                 held, held, state, state, state,
                 pltpu.VMEM((rows, HEAD_SIZE), jnp.float32),
                 pltpu.VMEM((1, queries.shape[1]), jnp.float32),
-                dma((q_heads,)), dma((kv_heads,)), dma((kv_heads,)),
+                pltpu.SMEM(span_mask.shape, jnp.int32),
+                pltpu.SMEM(section.shape, jnp.int32),
+                pltpu.VMEM(section_gate.shape, jnp.float32),
+                dma((3,)), dma((q_heads,)), dma((kv_heads,)), dma((kv_heads,)),
             ] + [dma((count, chunks))] * 6,
             compiler_params=pltpu.CompilerParams(
-                collective_id=0, has_side_effects=True, vmem_limit_bytes=40 * 2**20
+                collective_id=0, has_side_effects=True, vmem_limit_bytes=60*2**20
             ),
             name="span_attention",
         )(queries, keys, values, span_mask, section, section_gate)

time: 40 us -> 28.2 us (0.70)
  Pallas kernels: 32.5 us -> 25.9 us
  local copies, waits for them, and re-layouts: 6.55 us -> 1.48 us
    pallas_call x1, Pallas kernels: 32.5 us -> 25.9 us  [on_device(): pl.pallas_call(functools.partial(kernel, count, chunks), out_shape=(pltpu...]
    unnamed x14 -> x2, local copies, waits for them, and re-layouts: 6.55 us -> 1.48 us
where the time goes in v2:
time: 28.2 us; the launch traced here: 28 us
  Pallas kernels  25.9 us (92%)
  local copies, waits for them, and re-layouts  1.48 us (5%)
  between operations  0.64 us (2%)
    pallas_call x1, Pallas kernels, on_device(): pl.pallas_call(functools.partial(kernel, count, chunks), out_shape=(pltpu...  25.9 us
    unnamed x2, local copies, waits for them, and re-layouts  1.48 us

profile of v2, /device:TPU:24, one launch (start us, length us, event | category | flops | bytes accessed | tf_op | source)
XLA Modules:
  0.0 28.0 jit_solution(13220510550631900927)
XLA Ops:
  0.6 25.9 %span_attention.1 = (bf16[128,3072]{1,0:T(8,128)(2,1)S(1)}, f32[24,128]{1,0:T(8,128)S(1)}) custom-call(bf16[128,3072]{1,0:T(8,128)(2,1)} %q_hbm.1, bf16[128,512]{1,0:T(8,128)(2,1)} %k_hbm.1, bf16[128,512]{1,0:T(8,128)(2,1)} %v_hbm.1, s32[4,4]{1,0:T(4,128)} %mask_hbm.1, s32[4]{0:T(128)} %sec_hbm.1, f32[4,3072]{1,0:T(4,128)} %gate_hbm.1), custom_call_target="tpu_custom_call" | custom-call | tf_op jit(solution)/shard_map/span_attention/pallas_call | solution.py:280
  26.5 0.9 %copy.10 = bf16[128,3072]{1,0:T(8,128)(2,1)} copy(bf16[128,3072]{1,0:T(8,128)(2,1)S(1)} %get-tuple-element.2) | data formatting | bytes 1572864
  27.4 0.6 %copy.11 = f32[24,128]{1,0:T(8,128)} copy(f32[24,128]{1,0:T(8,128)S(1)} %get-tuple-element.3) | data formatting | bytes 24576

commit v3 on v2

--- a/solution.py
+++ b/solution.py
@@ -36,17 +36,6 @@
     has_prev = pair > 0
     has_next = pair < pairs - 1
 
-    def head_copy(src, dst, sem, head):
-        return pltpu.make_async_copy(
-            src.at[:, pl.ds(head * HEAD_SIZE, HEAD_SIZE)], dst, sem
-        )
-
-    own_k = [head_copy(k_hbm, kbuf.at[me, h], ksem.at[h], h) for h in range(kv_heads)]
-    own_v = [head_copy(v_hbm, vbuf.at[me, h], vsem.at[h], h) for h in range(kv_heads)]
-    own_q = [head_copy(q_hbm, qbuf.at[h], qsem.at[h], h) for h in range(q_heads)]
-    for copy in own_k + own_v:
-        copy.start()
-
     barrier = pltpu.get_barrier_semaphore()
     pl.semaphore_signal(barrier, inc=1, device_id={"tm": partner}, device_id_type=MESH)
 
@@ -58,13 +47,6 @@
     def _():
         pl.semaphore_signal(barrier, inc=1, device_id={"tm": me - 2}, device_id_type=MESH)
 
-    own_small = [
-        pltpu.make_async_copy(mask_hbm, mask_ref, small.at[0]),
-        pltpu.make_async_copy(sec_hbm, sec_ref, small.at[1]),
-        pltpu.make_async_copy(gate_hbm, gate_ref, small.at[2]),
-    ]
-    for copy in own_q + own_small:
-        copy.start()
     pl.semaphore_wait(
         barrier, 1 + has_next.astype(jnp.int32) + has_prev.astype(jnp.int32)
     )
@@ -92,23 +74,46 @@
     def v_over(slot, c):
         return send(vbuf, vy, vrecv, slot, c, partner)
 
-    for c in range(chunks):
-        for h in range(c * per, (c + 1) * per):
-            own_k[h].wait()
+    def first_send(src, buf, send_sem, recv_sem, c, target):
+        return pltpu.make_async_remote_copy(
+            src_ref=src.at[:, pl.ds(c * HEAD_SIZE, HEAD_SIZE)],
+            dst_ref=buf.at[me, c],
+            send_sem=send_sem.at[me, c],
+            recv_sem=recv_sem.at[me, c],
+            device_id={"tm": target},
+            device_id_type=MESH,
+        )
+
+    for c in range(kv_heads):
 
         @pl.when(has_next)
         def _():
-            k_on(me, c).start()
-
-        k_over(me, c).start()
-        for h in range(c * per, (c + 1) * per):
-            own_v[h].wait()
+            first_send(k_hbm, kbuf, kz, krecv, c, me + 2).start()
+
+        first_send(k_hbm, kbuf, ky, krecv, c, partner).start()
 
         @pl.when(has_next)
         def _():
-            v_on(me, c).start()
-
-        v_over(me, c).start()
+            first_send(v_hbm, vbuf, vz, vrecv, c, me + 2).start()
+
+        first_send(v_hbm, vbuf, vy, vrecv, c, partner).start()
+
+    def head_copy(src, dst, sem, head):
+        return pltpu.make_async_copy(
+            src.at[:, pl.ds(head * HEAD_SIZE, HEAD_SIZE)], dst, sem
+        )
+
+    own_k = [head_copy(k_hbm, kbuf.at[me, h], ksem.at[h], h) for h in range(kv_heads)]
+    own_v = [head_copy(v_hbm, vbuf.at[me, h], vsem.at[h], h) for h in range(kv_heads)]
+    own_q = [head_copy(q_hbm, qbuf.at[h], qsem.at[h], h) for h in range(q_heads)]
+    own_small = [
+        pltpu.make_async_copy(mask_hbm, mask_ref, small.at[0]),
+        pltpu.make_async_copy(sec_hbm, sec_ref, small.at[1]),
+        pltpu.make_async_copy(gate_hbm, gate_ref, small.at[2]),
+    ]
+    own_all = own_small + own_k + own_v + own_q
+    for copy in own_all:
+        copy.start()
 
     def visit(slots, head, first, last):
         allowed = [mask_ref[pair, slot // 2] > 0 for slot in slots]
@@ -176,9 +181,7 @@
                 sums = jnp.where(lane == j, log_total[cut], sums)
         ltm_s[...] = sums
 
-    for copy in own_q:
-        copy.wait()
-    for copy in own_small:
+    for copy in own_all:
         copy.wait()
 
     def own(head, carry):
@@ -239,6 +242,16 @@
     lax.fori_loop(0, kv_heads, end, 0)
     lt_ref[...] = jnp.transpose(ltm_s[...])[:q_heads]
 
+    for c in range(kv_heads):
+
+        @pl.when(has_next)
+        def _():
+            first_send(k_hbm, kbuf, kz, krecv, c, me + 2).wait_send()
+            first_send(v_hbm, vbuf, vz, vrecv, c, me + 2).wait_send()
+
+        first_send(k_hbm, kbuf, ky, krecv, c, partner).wait_send()
+        first_send(v_hbm, vbuf, vy, vrecv, c, partner).wait_send()
+
     def settle(i, carry):
         slot = me - 2 * i
         for c in range(chunks):
@@ -250,18 +263,35 @@
 
             k_over(slot, c).wait_send()
 
-            @pl.when((slot >= 2) | (i == 0))
+            @pl.when(slot >= 2)
             def _():
                 v_over(slot, c).wait_send()
 
         return carry
 
-    lax.fori_loop(0, pair + 1, settle, 0)
+    lax.fori_loop(1, pair + 1, settle, 0)
 
     @pl.when(has_next)
     def _():
         for c in range(chunks):
             v_on(far, c).wait_send()
+
+
+def finish(mixed_ref, log_ref, mixed_out, log_out, sem):
+    parts = sem.shape[0] - 1
+    high = mixed_ref.shape[0] // parts
+    copies = [
+        pltpu.make_async_copy(
+            mixed_ref.at[pl.ds(i * high, high)],
+            mixed_out.at[pl.ds(i * high, high)],
+            sem.at[i],
+        )
+        for i in range(parts)
+    ] + [pltpu.make_async_copy(log_ref, log_out, sem.at[parts])]
+    for copy in copies:
+        copy.start()
+    for copy in copies:
+        copy.wait()
 
 
 def solution(mesh):
@@ -275,9 +305,10 @@
         chunks = kv_heads
         vmem = pl.BlockSpec(memory_space=pltpu.VMEM)
         dma = pltpu.SemaphoreType.DMA
+        keep_near = lambda x: pltpu.with_memory_space_constraint(x, pltpu.VMEM)
         state = pltpu.VMEM((q_heads, rows, HEAD_SIZE), jnp.float32)
         held = pltpu.VMEM((count, kv_heads, rows, HEAD_SIZE), jnp.bfloat16)
-        return pl.pallas_call(
+        mixed, log_total = pl.pallas_call(
             functools.partial(kernel, count, chunks),
             out_shape=(
                 pltpu.VMEM(queries.shape, jnp.bfloat16),
@@ -300,6 +331,18 @@
             ),
             name="span_attention",
         )(queries, keys, values, span_mask, section, section_gate)
+        return pl.pallas_call(
+            finish,
+            out_shape=(
+                jax.ShapeDtypeStruct(mixed.shape, mixed.dtype),
+                jax.ShapeDtypeStruct(log_total.shape, log_total.dtype),
+            ),
+            in_specs=[vmem, vmem],
+            out_specs=[pl.BlockSpec(memory_space=pltpu.HBM)] * 2,
+            scratch_shapes=[dma((5,))],
+            compiler_params=pltpu.CompilerParams(vmem_limit_bytes=4 * 2**20),
+            name="write_back",
+        )(keep_near(mixed), keep_near(log_total))
 
     placed = (
         P(("grp", "tm"), "head"),

time: 28.2 us -> 27.9 us (0.989)
  local copies, waits for them, and re-layouts: 1.48 us -> 0 us
  Pallas kernels: 25.9 us -> 27 us
    unnamed x2 -> x0, local copies, waits for them, and re-layouts: 1.48 us -> none
    pallas_call x0 -> x1, Pallas kernels: none -> 0.92 us  [on_device(): pl.pallas_call(finish, out_shape=(jax.ShapeDtypeStruct(mixed.shape, mixed...]
where the time goes in v3:
time: 27.9 us; the launch traced here: 27.7 us
  Pallas kernels  27 us (97%)
  between operations  0.64 us (2%)
    pallas_call x1, Pallas kernels, on_device(): pl.pallas_call(functools.partial(kernel, count, chunks), out_shape=(pltpu...  26.1 us
    pallas_call x1, Pallas kernels, on_device(): pl.pallas_call(finish, out_shape=(jax.ShapeDtypeStruct(mixed.shape, mixed...  0.92 us

profile of v3, /device:TPU:24, one launch (start us, length us, event | category | flops | bytes accessed | tf_op | source)
XLA Modules:
  0.0 27.7 jit_solution(1040607449589633416)
XLA Ops:
  0.6 26.1 %span_attention.1 = (bf16[128,3072]{1,0:T(8,128)(2,1)S(1)}, f32[24,128]{1,0:T(8,128)S(1)}) custom-call(bf16[128,3072]{1,0:T(8,128)(2,1)} %q_hbm.1, bf16[128,512]{1,0:T(8,128)(2,1)} %k_hbm.1, bf16[128,512]{1,0:T(8,128)(2,1)} %v_hbm.1, s32[4,4]{1,0:T(4,128)} %mask_hbm.1, s32[4]{0:T(128)} %sec_hbm.1, f32[4,3072]{1,0:T(4,128)} %gate_hbm.1), custom_call_target="tpu_custom_call" | custom-call | tf_op jit(solution)/shard_map/span_attention/pallas_call | solution.py:311
  26.7 0.9 %write_back.1 = (bf16[128,3072]{1,0:T(8,128)(2,1)}, f32[24,128]{1,0:T(8,128)}) custom-call(bf16[128,3072]{1,0:T(8,128)(2,1)S(1)} %get-tuple-element.4.mixed_ref, f32[24,128]{1,0:T(8,128)S(1)} %get-tuple-element.5.log_ref), custom_call_target="tpu_custom_call" | custom-call | tf_op jit(solution)/shard_map/write_back/pallas_call | solution.py:334

commit v4 on v3

--- a/solution.py
+++ b/solution.py
@@ -91,6 +91,8 @@
             first_send(k_hbm, kbuf, kz, krecv, c, me + 2).start()
 
         first_send(k_hbm, kbuf, ky, krecv, c, partner).start()
+
+    for c in range(kv_heads):
 
         @pl.when(has_next)
         def _():
@@ -199,14 +201,19 @@
         behind = me - 2 * i
         across = partner - 2 * (i - 1)
 
+        def pass_keys(c, inner):
+            k_on(behind, c).wait_recv()
+
+            @pl.when(has_next)
+            def _():
+                k_on(behind, c).start()
+
+            k_over(behind, c).start()
+            return inner
+
+        lax.fori_loop(0, kv_heads, pass_keys, 0)
+
         def at_head(c, inner):
-            k_on(behind, c).wait_recv()
-
-            @pl.when(has_next)
-            def _():
-                k_on(behind, c).start()
-
-            k_over(behind, c).start()
             v_on(behind, c).wait_recv()
 
             @pl.when(has_next)

time: 27.9 us -> 27.4 us (0.982)
  Pallas kernels: 27 us -> 26.5 us
    pallas_call x1, Pallas kernels: 26.1 us -> 25.6 us  [on_device(): pl.pallas_call(functools.partial(kernel, count, chunks), out_shape=(pltpu...]
where the time goes in v4:
time: 27.4 us; the launch traced here: 27.2 us
  Pallas kernels  26.5 us (97%)
  between operations  0.64 us (2%)
    pallas_call x1, Pallas kernels, on_device(): pl.pallas_call(functools.partial(kernel, count, chunks), out_shape=(pltpu...  25.6 us
    pallas_call x1, Pallas kernels, on_device(): pl.pallas_call(finish, out_shape=(jax.ShapeDtypeStruct(mixed.shape, mixed...  0.92 us

profile of v4, /device:TPU:24, one launch (start us, length us, event | category | flops | bytes accessed | tf_op | source)
XLA Modules:
  0.0 27.2 jit_solution(955858131931865866)
XLA Ops:
  0.6 25.6 %span_attention.1 = (bf16[128,3072]{1,0:T(8,128)(2,1)S(1)}, f32[24,128]{1,0:T(8,128)S(1)}) custom-call(bf16[128,3072]{1,0:T(8,128)(2,1)} %q_hbm.1, bf16[128,512]{1,0:T(8,128)(2,1)} %k_hbm.1, bf16[128,512]{1,0:T(8,128)(2,1)} %v_hbm.1, s32[4,4]{1,0:T(4,128)} %mask_hbm.1, s32[4]{0:T(128)} %sec_hbm.1, f32[4,3072]{1,0:T(4,128)} %gate_hbm.1), custom_call_target="tpu_custom_call" | custom-call | tf_op jit(solution)/shard_map/span_attention/pallas_call | solution.py:318
  26.2 0.9 %write_back.1 = (bf16[128,3072]{1,0:T(8,128)(2,1)}, f32[24,128]{1,0:T(8,128)}) custom-call(bf16[128,3072]{1,0:T(8,128)(2,1)S(1)} %get-tuple-element.4.mixed_ref, f32[24,128]{1,0:T(8,128)S(1)} %get-tuple-element.5.log_ref), custom_call_target="tpu_custom_call" | custom-call | tf_op jit(solution)/shard_map/write_back/pallas_call | solution.py:341

commit v5 on v4

--- a/solution.py
+++ b/solution.py
@@ -235,20 +235,6 @@
 
     far = 1 - side
 
-    def end(c, carry):
-        v_on(far, c).wait_recv()
-
-        @pl.when(has_next)
-        def _():
-            v_on(far, c).start()
-
-        k_over(far, c).wait_recv()
-        visit([far], c, False, True)
-        return carry
-
-    lax.fori_loop(0, kv_heads, end, 0)
-    lt_ref[...] = jnp.transpose(ltm_s[...])[:q_heads]
-
     for c in range(kv_heads):
 
         @pl.when(has_next)
@@ -276,7 +262,23 @@
 
         return carry
 
-    lax.fori_loop(1, pair + 1, settle, 0)
+    lax.fori_loop(1, pair, settle, 0)
+
+    def end(c, carry):
+        v_on(far, c).wait_recv()
+
+        @pl.when(has_next)
+        def _():
+            v_on(far, c).start()
+
+        k_over(far, c).wait_recv()
+        visit([far], c, False, True)
+        return carry
+
+    lax.fori_loop(0, kv_heads, end, 0)
+    lt_ref[...] = jnp.transpose(ltm_s[...])[:q_heads]
+
+    lax.fori_loop(jnp.maximum(pair, 1), pair + 1, settle, 0)
 
     @pl.when(has_next)
     def _():

time: 27.4 us -> 27.3 us (level)
  no operation moved by 1% of the time
where the time goes in v5:
time: 27.3 us; the launch traced here: 27.1 us
  Pallas kernels  26.5 us (97%)
  between operations  0.64 us (2%)
    pallas_call x1, Pallas kernels, on_device(): pl.pallas_call(functools.partial(kernel, count, chunks), out_shape=(pltpu...  25.6 us
    pallas_call x1, Pallas kernels, on_device(): pl.pallas_call(finish, out_shape=(jax.ShapeDtypeStruct(mixed.shape, mixed...  0.92 us

profile of v5, /device:TPU:24, one launch (start us, length us, event | category | flops | bytes accessed | tf_op | source)
XLA Modules:
  0.0 27.1 jit_solution(6358818570742334995)
XLA Ops:
  0.6 25.6 %span_attention.1 = (bf16[128,3072]{1,0:T(8,128)(2,1)S(1)}, f32[24,128]{1,0:T(8,128)S(1)}) custom-call(bf16[128,3072]{1,0:T(8,128)(2,1)} %q_hbm.1, bf16[128,512]{1,0:T(8,128)(2,1)} %k_hbm.1, bf16[128,512]{1,0:T(8,128)(2,1)} %v_hbm.1, s32[4,4]{1,0:T(4,128)} %mask_hbm.1, s32[4]{0:T(128)} %sec_hbm.1, f32[4,3072]{1,0:T(4,128)} %gate_hbm.1), custom_call_target="tpu_custom_call" | custom-call | tf_op jit(solution)/shard_map/span_attention/pallas_call | solution.py:320
  26.2 0.9 %write_back.1 = (bf16[128,3072]{1,0:T(8,128)(2,1)}, f32[24,128]{1,0:T(8,128)}) custom-call(bf16[128,3072]{1,0:T(8,128)(2,1)S(1)} %get-tuple-element.4.mixed_ref, f32[24,128]{1,0:T(8,128)S(1)} %get-tuple-element.5.log_ref), custom_call_target="tpu_custom_call" | custom-call | tf_op jit(solution)/shard_map/write_back/pallas_call | solution.py:343
